TPU v7x, 32 devices: a whole 2x2x4 slice. The times are simulated.
32 devices in a mesh: section: 2 (over core), seq: 16 (over z, y, x).
Axes of the slice: x: 2, y: 2, z: 4, core: 2. Of those that a mesh axis runs over, the one named last changes fastest.
Arguments:
- queries: bfloat16 [4096, 4096], P('seq', 'section'), may hold values from -50 to 50
- key_rows: bfloat16 [4096, 4096], P('seq', 'section'), may hold values from -6 to 6
- value_rows: bfloat16 [4096, 4096], P('seq', 'section'), may hold values from -6 to 6
- block_pattern: int32 [32, 8], P('seq'), may hold values from 0 to 1, as said below
- out_weight: bfloat16 [4096, 4096], P('section'), may hold values from -0.09375 to 0.09375
- hidden: bfloat16 [4096, 4096], P('seq', 'section'), may hold values from -3 to 3
- norm_gain: float32 [4096], P('section'), may hold values from 0.5 to 1.5
Outputs:
- stream_out: bfloat16 [4096, 4096], P('seq', 'section')
- normed: bfloat16 [4096, 4096], P('seq', 'section')
Inputs may be any that keep to these rules, and one draw needn't show every extreme that they name: `block_pattern`: column 0 is 1 in every row: every query block attends its own block.
All inputs are finite; a program needn't handle non-finite values.
Results may differ from a plain program's by a relative error of at most 0.008.
Values may be sent and summed in bfloat16 or wider, within the bound.
A program may use at most 128 MiB of HBM per device.

v0:
```python
import math

import jax
import jax.numpy as jnp
from jax import lax
from jax.sharding import PartitionSpec as P

HEAD_DIM = 128
BLOCK = 128
WINDOW_BLOCKS = 8
BLK_DEV = 2


def from_behind(block, axis, distance):
    devices = range(lax.axis_size(axis))
    route = [(i - distance, i) for i in devices if i - distance in devices]
    return lax.ppermute(block, axis, route)


def window_mask(block_pattern, shard_index):
    key_blocks = WINDOW_BLOCKS - 1 + BLK_DEV
    query_block = jnp.arange(BLK_DEV, dtype=jnp.int32)[:, None]
    key_block = jnp.arange(key_blocks, dtype=jnp.int32)[None, :]
    offsets = query_block + (WINDOW_BLOCKS - 1) - key_block
    matches = offsets[:, :, None] == jnp.arange(WINDOW_BLOCKS, dtype=jnp.int32)[None, None, :]
    allowed = jnp.any(matches & (block_pattern[:, None, :] == 1), axis=2)
    global_key = shard_index * BLK_DEV - (WINDOW_BLOCKS - 1) + key_block
    allowed = allowed & (global_key >= 0)
    row_allowed = jnp.repeat(jnp.repeat(allowed, BLOCK, axis=0), BLOCK, axis=1)
    row_offsets = jnp.repeat(jnp.repeat(offsets, BLOCK, axis=0), BLOCK, axis=1)
    query_place = (jnp.arange(BLK_DEV * BLOCK, dtype=jnp.int32) % BLOCK)[:, None]
    key_place = (jnp.arange(key_blocks * BLOCK, dtype=jnp.int32) % BLOCK)[None, :]
    causal = (row_offsets > 0) | (key_place <= query_place)
    return row_allowed & causal


def attend(query_rows, key_all, value_all, visible):
    row_count = query_rows.shape[0]
    heads_here = query_rows.shape[1] // HEAD_DIM
    front_rows = (WINDOW_BLOCKS - 1) * BLOCK
    block_rows = math.gcd(row_count, 512)
    scaling = 1.0 / math.sqrt(HEAD_DIM)
    key_span = front_rows + block_rows
    query_group = query_rows.reshape(block_rows, heads_here, HEAD_DIM)
    key_group = key_all.reshape(key_span, heads_here, HEAD_DIM)
    value_group = value_all.reshape(key_span, heads_here, HEAD_DIM)
    scores = (
        jnp.einsum("qhd,khd->hqk", query_group, key_group, preferred_element_type=jnp.float32)
        * scaling
    )
    scores = jnp.where(visible[None], scores, -jnp.inf)
    largest = jnp.max(scores, axis=2, keepdims=True)
    exponent = jnp.exp(scores - largest)
    weights = (exponent / jnp.sum(exponent, axis=2, keepdims=True)).astype(jnp.bfloat16)
    mixture = jnp.einsum("hqk,khd->qhd", weights, value_group, preferred_element_type=jnp.float32)
    results = mixture.reshape(block_rows, heads_here * HEAD_DIM)
    return results.astype(jnp.bfloat16)


def shards(queries, key_rows, value_rows, block_pattern, out_weight, hidden, norm_gain):
    shard_index = lax.axis_index("seq")
    reach_count = (WINDOW_BLOCKS - 2) // BLK_DEV + 1
    tail_rows = (WINDOW_BLOCKS - 1 - (reach_count - 1) * BLK_DEV) * BLOCK
    received = []
    for offset in range(1, reach_count + 1):
        if offset == reach_count:
            outgoing = (
                key_rows[key_rows.shape[0] - tail_rows :],
                value_rows[value_rows.shape[0] - tail_rows :],
            )
        else:
            outgoing = (key_rows, value_rows)
        received.append(from_behind((outgoing[0], outgoing[1]), "seq", offset))
    ordered = received[::-1]
    key_all = jnp.concatenate([couple[0] for couple in ordered] + [key_rows], 0)
    value_all = jnp.concatenate([couple[1] for couple in ordered] + [value_rows], 0)
    visible = window_mask(block_pattern, shard_index)
    attended = attend(queries, key_all, value_all, visible)
    partial_value = jnp.dot(attended, out_weight, preferred_element_type=jnp.float32)
    projected = lax.psum_scatter(
        partial_value.astype(jnp.bfloat16), "section", scatter_dimension=0, tiled=True
    ).astype(jnp.float32)
    hidden_full = lax.all_to_all(hidden, "section", split_axis=0, concat_axis=1, tiled=True)
    gain_full = lax.all_gather(norm_gain, "section", axis=0, tiled=True)
    stream = hidden_full.astype(jnp.float32) + projected
    mean_square = jnp.mean(stream * stream, axis=1, keepdims=True)
    normed = stream * lax.rsqrt(mean_square + 1e-06) * gain_full[None, :]
    stream_cols, normed_cols = (
        lax.all_to_all(
            stream.astype(jnp.bfloat16), "section", split_axis=1, concat_axis=0, tiled=True
        ),
        lax.all_to_all(
            normed.astype(jnp.bfloat16), "section", split_axis=1, concat_axis=0, tiled=True
        ),
    )
    return (stream_cols, normed_cols)


def solution(mesh):
    placed = (
        P("seq", "section"),
        P("seq", "section"),
        P("seq", "section"),
        P("seq", None),
        P("section", None),
        P("seq", "section"),
        P("section"),
    )
    return jax.shard_map(
        shards,
        mesh=mesh,
        in_specs=placed,
        out_specs=(P("seq", "section"), P("seq", "section")),
        check_vma=False,
    )
```

profile of v0, /device:TPU:9, one launch (start us, length us, event | category | flops | bytes accessed | tf_op | source)
XLA Modules:
  0.0 238.6 jit_solution(11054848941124161800)
XLA Ops:
  7.2 0.0 copy-start
  7.2 0.0 copy-start.3
  7.2 0.0 reduce-scatter.2.cloned.1.call-start
  7.2 1.6 copy.46
  8.9 4.1 %collective-permute-start.5 = (bf16[256,2048]{0,1:T(8,128)(2,1)S(1)}, bf16[256,2048]{0,1:T(8,128)(2,1)}, u32[]{:S(2)}, u32[]{:S(2)}) collective-permute-start(bf16[256,2048]{0,1:T(8,128)(2,1)S(1)} %copy.46), channel_id=1, source_target_pairs={{0,3},{1,4},{2,5},{3,6},{4,7},{5,8},{6,9},{7,10},{8,11},{9,12},{10... | collective-permute-start | bytes 3145736 | tf_op jit(solution)/shard_map/ppermute | solution.py:17
  12.9 3.1 %collective-permute-start.6 = (bf16[256,2048]{0,1:T(8,128)(2,1)S(1)}, bf16[256,2048]{0,1:T(8,128)(2,1)}, u32[]{:S(2)}, u32[]{:S(2)}) collective-permute-start(bf16[256,2048]{0,1:T(8,128)(2,1)S(1)} %copy.46), channel_id=1, source_target_pairs={{0,2},{1,3},{2,4},{3,5},{4,6},{5,7},{6,8},{7,9},{8,10},{9,11},{10,... | collective-permute-start | bytes 3145736 | tf_op jit(solution)/shard_map/ppermute | solution.py:17
  16.1 2.2 collective-permute-start.7
  18.3 0.8 slice.8
  19.2 3.2 %collective-permute-start.4 = (bf16[128,2048]{0,1:T(8,128)(2,1)}, bf16[128,2048]{0,1:T(8,128)(2,1)}, u32[]{:S(2)}, u32[]{:S(2)}) collective-permute-start(bf16[128,2048]{0,1:T(8,128)(2,1)} %slice.8), channel_id=1, source_target_pairs={{0,4},{1,5},{2,6},{3,7},{4,8},{5,9},{6,10},{7,11},{8,12},{9,13},{1... | collective-permute-start | bytes 1572872 | tf_op jit(solution)/shard_map/ppermute | solution.py:17
  22.4 1.9 slice.6
  24.2 1.9 collective-permute-start
  26.2 0.1 copy.44
  26.3 0.7 broadcast_compare_fusion.1
  27.0 0.1 fusion.18
  27.1 0.1 copy.45
  27.2 0.1 broadcast_bitcast_fusion.1
  27.3 0.1 broadcast_bitcast_fusion
  27.4 0.3 fusion.7
  27.8 5.9 %collective-permute-done.4 = bf16[128,2048]{0,1:T(8,128)(2,1)} collective-permute-done((bf16[128,2048]{0,1:T(8,128)(2,1)}, bf16[128,2048]{0,1:T(8,128)(2,1)}, u32[]{:S(2)}, u32[]{:S(2)}) %collective-permute-start.4) | collective-permute-done | bytes 524320 | tf_op jit(solution)/shard_map/ppermute | solution.py:17
  33.7 62.3 %collective-permute-start.1 = (bf16[256,2048]{1,0:T(8,128)(2,1)}, bf16[256,2048]{1,0:T(8,128)(2,1)S(1)}, u32[]{:S(2)}, u32[]{:S(2)}) collective-permute-start(bf16[256,2048]{1,0:T(8,128)(2,1)} %param.9), channel_id=1, source_target_pairs={{0,3},{1,4},{2,5},{3,6},{4,7},{5,8},{6,9},{7,10},{8,11},{9,12},{10... | collective-permute-start | bytes 3145736 | tf_op jit(solution)/shard_map/ppermute | solution.py:17
  96.0 1.1 constant_dynamic-update-slice_fusion.9
  97.2 0.0 collective-permute-done
  97.2 0.0 copy-done.3
  97.2 1.9 collective-permute-start.2
  99.1 1.9 constant_dynamic-update-slice_fusion.4
  101.0 0.0 collective-permute-done.5
  101.0 10.3 %collective-permute-start.3 = (bf16[256,2048]{1,0:T(8,128)(2,1)S(1)}, bf16[256,2048]{1,0:T(8,128)(2,1)}, u32[]{:S(2)}, u32[]{:S(2)}) collective-permute-start(bf16[256,2048]{1,0:T(8,128)(2,1)S(1)} %copy-done.3), channel_id=1, source_target_pairs={{0,1},{1,2},{2,3},{3,4},{4,5},{5,6},{6,7},{7,8},{8,9},{9,10},{10,1... | collective-permute-start | bytes 3145736 | tf_op jit(solution)/shard_map/ppermute | solution.py:17
  111.4 1.3 constant_dynamic-update-slice_fusion.8
  112.7 0.0 collective-permute-done.6
  112.7 1.3 constant_dynamic-update-slice_fusion.7
  114.0 0.0 collective-permute-done.7
  114.0 1.3 constant_dynamic-update-slice_fusion.6
  115.3 0.1 constant_dynamic-update-slice_fusion.5
  115.3 0.0 copy-start.2
  115.4 0.9 collective-permute-done.1
  116.2 1.7 constant_dynamic-update-slice_fusion.3
  117.9 0.0 copy-done
  117.9 7.9 %convolution_multiply_fusion = f32[16,1152,256]{2,1,0:T(8,128)} fusion(bf16[1152,16,128]{0,2,1:T(8,128)(2,1)S(1)} %bitcast.76, bf16[256,2048]{1,0:T(8,128)(2,1)S(1)} %copy-done), kind=kOutput, calls=%fused_computation.2 | convolution fusion | flops 1212678144 | bytes 24641536 | tf_op jit(solution)/shard_map/qhd,khd->hqk/dot_general | solution.py:48
  125.8 15.6 %collective-permute-done.2 = bf16[256,2048]{1,0:T(8,128)(2,1)S(1)} collective-permute-done((bf16[256,2048]{1,0:T(8,128)(2,1)S(1)}, bf16[256,2048]{1,0:T(8,128)(2,1)S(1)}, u32[]{:S(2)}, u32[]{:S(2)}) %collective-permute-start.2) | collective-permute-done | bytes 1048608 | tf_op jit(solution)/shard_map/ppermute | solution.py:17
  141.4 1.1 constant_dynamic-update-slice_fusion.2
  142.5 8.2 %exponential_reduce_fusion = f32[16,256]{1,0:T(8,128)S(1)} fusion(pred[256,1152]{0,1:T(8,128)(4,1)S(1)} %fusion.7, bf16[1152,16,128]{0,2,1:T(8,128)(2,1)} %bitcast.77, bf16[256,2048]{1,0:T(8,128)(2,1)S(1)} %copy-done), kind=kOutput, calls=%fused_computation.6 | convolution fusion | flops 1226835072 | bytes 6078464 | tf_op jit(solution)/shard_map/sub | solution.py:53
  150.7 21.8 %collective-permute-done.3 = bf16[256,2048]{1,0:T(8,128)(2,1)} collective-permute-done((bf16[256,2048]{1,0:T(8,128)(2,1)S(1)}, bf16[256,2048]{1,0:T(8,128)(2,1)}, u32[]{:S(2)}, u32[]{:S(2)}) %collective-permute-start.3) | collective-permute-done | bytes 1048608 | tf_op jit(solution)/shard_map/ppermute | solution.py:17
  172.5 2.4 constant_dynamic-update-slice_fusion.1
  174.8 1.1 constant_dynamic-update-slice_fusion
  175.9 6.7 %copy.43 = bf16[1152,2048]{0,1:T(8,128)(2,1)} copy(bf16[1152,2048]{1,0:T(8,128)(2,1)} %constant_dynamic-update-slice_fusion) | data formatting | bytes 9437184 | tf_op jit(solution)/shard_map/concatenate | solution.py:76
  182.6 12.0 %fusion.6 = bf16[16,128,256]{2,1,0:T(8,128)(2,1)S(1)} fusion(bf16[1152,16,128]{0,2,1:T(8,128)(2,1)} %bitcast.78, f32[16,256]{1,0:T(8,128)S(1)} %exponential_reduce_fusion, f32[16,1152,256]{2,1,0:T(8,128)} %convolution_multiply_fusion, pred[256,1152]{0,1:T(8,128)(4,1)S(1)} %fusion.7), kind=kOutput, calls=%fused_computation.15 | convolution fusion | flops 1227363456 | bytes 24952832 | tf_op jit(solution)/shard_map/hqk,khd->qhd/dot_general | solution.py:55
  194.7 0.0 copy-start.4
  194.7 11.7 %convolution_convert_fusion = bf16[256,4096]{1,0:T(8,128)(2,1)} fusion(bf16[256,2048]{0,1:T(8,128)(2,1)S(1)} %bitcast.85, bf16[2048,4096]{1,0:T(8,128)(2,1)} %param.11), kind=kOutput, calls=%fused_computation.10 | convolution fusion | flops 4296015872 | bytes 19922944 | tf_op jit(solution)/shard_map/dot_general | solution.py:79
  206.3 0.0 reduce-scatter.2.cloned.1.call-update
  206.4 0.0 copy-start.5
  206.4 5.7 %all_to_all.51 = bf16[2,128,2048]{2,1,0:T(8,128)(2,1)S(1)} all-to-all(bf16[2,128,2048]{2,1,0:T(8,128)(2,1)S(1)} %bitcast.86), channel_id=1, replica_groups=mesh['section'=2,'seq'=16] {'section'}, dimensions={0} | all-to-all | bytes 2097152 | tf_op jit(solution)/shard_map/all_to_all | solution.py:83
  212.1 0.2 convert_bitcast_fusion
  212.3 0.2 copy.61
  212.6 1.8 all_gather.3
  214.4 2.6 %reduce-scatter.2.cloned.1.call-done = bf16[128,4096]{1,0:T(8,128)(2,1)} async-done(((bf16[256,4096]{1,0:T(8,128)(2,1)}), bf16[128,4096]{1,0:T(8,128)(2,1)}) %reduce-scatter.2.cloned.1.call-update) | async-done | bytes 1048592 | tf_op jit(solution)/shard_map/reduce_scatter | solution.py:80
  217.1 1.6 multiply_reduce_fusion
  218.7 1.6 multiply_convert_fusion
  220.3 0.1 copy.78
  220.4 0.0 copy-start.1
  220.4 4.7 %all_to_all.52 = bf16[128,2,2048]{2,0,1:T(8,128)(2,1)S(1)} all-to-all(bf16[128,2,2048]{2,0,1:T(8,128)(2,1)S(1)} %bitcast.81), channel_id=1, replica_groups=mesh['section'=2,'seq'=16] {'section'}, dimensions={1} | all-to-all | bytes 2097152 | tf_op jit(solution)/shard_map/all_to_all | solution.py:89
  225.1 0.1 copy.77
  225.2 4.6 %all_to_all.53 = bf16[128,2,2048]{2,0,1:T(8,128)(2,1)S(1)} all-to-all(bf16[128,2,2048]{2,0,1:T(8,128)(2,1)S(1)} %bitcast.82), channel_id=1, replica_groups=mesh['section'=2,'seq'=16] {'section'}, dimensions={1} | all-to-all | bytes 2097152 | tf_op jit(solution)/shard_map/all_to_all | solution.py:92
  229.8 1.0 copy.89
  230.7 1.0 copy.90
  (16 shorter events, 0.1 us)
Async XLA Ops:
  7.2 110.7 %copy-start = (bf16[256,2048]{1,0:T(8,128)(2,1)S(1)}, bf16[256,2048]{1,0:T(8,128)(2,1)}, u32[]{:S(2)}) copy-start(bf16[256,2048]{1,0:T(8,128)(2,1)} %param.7) | copy-start | bytes 3145732
  7.2 90.0 %copy-start.3 = (bf16[256,2048]{1,0:T(8,128)(2,1)S(1)}, bf16[256,2048]{1,0:T(8,128)(2,1)}, u32[]{:S(2)}) copy-start(bf16[256,2048]{1,0:T(8,128)(2,1)} %param.9) | copy-start | bytes 3145732
  7.2 209.9 %reduce-scatter.2.cloned.1.call-start = ((), (), s32[]{:S(2)}) async-start(), calls=%async_computation.4 | async-start | bytes 3145728 | tf_op jit(solution)/shard_map/reduce_scatter | solution.py:80
  8.9 92.2 %collective-permute-start.5 = (bf16[256,2048]{0,1:T(8,128)(2,1)S(1)}, bf16[256,2048]{0,1:T(8,128)(2,1)}, u32[]{:S(2)}, u32[]{:S(2)}) collective-permute-start(bf16[256,2048]{0,1:T(8,128)(2,1)S(1)} %copy.46), channel_id=1, source_target_pairs={{0,3},{1,4},{2,5},{3,6},{4,7},{5,8},{6,9},{7,10},{8,11},{9,12},{10... | collective-permute-start | bytes 3145736 | tf_op jit(solution)/shard_map/ppermute | solution.py:17
  12.9 99.7 %collective-permute-start.6 = (bf16[256,2048]{0,1:T(8,128)(2,1)S(1)}, bf16[256,2048]{0,1:T(8,128)(2,1)}, u32[]{:S(2)}, u32[]{:S(2)}) collective-permute-start(bf16[256,2048]{0,1:T(8,128)(2,1)S(1)} %copy.46), channel_id=1, source_target_pairs={{0,2},{1,3},{2,4},{3,5},{4,6},{5,7},{6,8},{7,9},{8,10},{9,11},{10,... | collective-permute-start | bytes 3145736 | tf_op jit(solution)/shard_map/ppermute | solution.py:17
  16.1 97.9 %collective-permute-start.7 = (bf16[256,2048]{0,1:T(8,128)(2,1)S(1)}, bf16[256,2048]{0,1:T(8,128)(2,1)}, u32[]{:S(2)}, u32[]{:S(2)}) collective-permute-start(bf16[256,2048]{0,1:T(8,128)(2,1)S(1)} %copy.46), channel_id=1, source_target_pairs={{0,1},{1,2},{2,3},{3,4},{4,5},{5,6},{6,7},{7,8},{8,9},{9,10},{10,1... | collective-permute-start | bytes 3145736 | tf_op jit(solution)/shard_map/ppermute | solution.py:17
  19.2 14.5 %collective-permute-start.4 = (bf16[128,2048]{0,1:T(8,128)(2,1)}, bf16[128,2048]{0,1:T(8,128)(2,1)}, u32[]{:S(2)}, u32[]{:S(2)}) collective-permute-start(bf16[128,2048]{0,1:T(8,128)(2,1)} %slice.8), channel_id=1, source_target_pairs={{0,4},{1,5},{2,6},{3,7},{4,8},{5,9},{6,10},{7,11},{8,12},{9,13},{1... | collective-permute-start | bytes 1572872 | tf_op jit(solution)/shard_map/ppermute | solution.py:17
  24.2 72.9 %collective-permute-start = (bf16[128,2048]{1,0:T(8,128)(2,1)}, bf16[128,2048]{1,0:T(8,128)(2,1)}, u32[]{:S(2)}, u32[]{:S(2)}) collective-permute-start(bf16[128,2048]{1,0:T(8,128)(2,1)} %slice.6), channel_id=1, source_target_pairs={{0,4},{1,5},{2,6},{3,7},{4,8},{5,9},{6,10},{7,11},{8,12},{9,13},{1... | collective-permute-start | bytes 1572872 | tf_op jit(solution)/shard_map/ppermute | solution.py:17
  33.7 82.5 %collective-permute-start.1 = (bf16[256,2048]{1,0:T(8,128)(2,1)}, bf16[256,2048]{1,0:T(8,128)(2,1)S(1)}, u32[]{:S(2)}, u32[]{:S(2)}) collective-permute-start(bf16[256,2048]{1,0:T(8,128)(2,1)} %param.9), channel_id=1, source_target_pairs={{0,3},{1,4},{2,5},{3,6},{4,7},{5,8},{6,9},{7,10},{8,11},{9,12},{10... | collective-permute-start | bytes 3145736 | tf_op jit(solution)/shard_map/ppermute | solution.py:17
  97.2 44.2 %collective-permute-start.2 = (bf16[256,2048]{1,0:T(8,128)(2,1)S(1)}, bf16[256,2048]{1,0:T(8,128)(2,1)S(1)}, u32[]{:S(2)}, u32[]{:S(2)}) collective-permute-start(bf16[256,2048]{1,0:T(8,128)(2,1)S(1)} %copy-done.3), channel_id=1, source_target_pairs={{0,2},{1,3},{2,4},{3,5},{4,6},{5,7},{6,8},{7,9},{8,10},{9,11},{10,... | collective-permute-start | bytes 3145736 | tf_op jit(solution)/shard_map/ppermute | solution.py:17
  101.0 71.5 %collective-permute-start.3 = (bf16[256,2048]{1,0:T(8,128)(2,1)S(1)}, bf16[256,2048]{1,0:T(8,128)(2,1)}, u32[]{:S(2)}, u32[]{:S(2)}) collective-permute-start(bf16[256,2048]{1,0:T(8,128)(2,1)S(1)} %copy-done.3), channel_id=1, source_target_pairs={{0,1},{1,2},{2,3},{3,4},{4,5},{5,6},{6,7},{7,8},{8,9},{9,10},{10,1... | collective-permute-start | bytes 3145736 | tf_op jit(solution)/shard_map/ppermute | solution.py:17
  115.3 10.5 %copy-start.2 = (bf16[1152,2048]{0,1:T(8,128)(2,1)}, bf16[1152,2048]{0,1:T(8,128)(2,1)S(1)}, u32[]{:S(2)}) copy-start(bf16[1152,2048]{0,1:T(8,128)(2,1)S(1)} %constant_dynamic-update-slice_fusion.5) | copy-start | bytes 14155780
  194.7 11.7 %copy-start.4 = (bf16[256,2048]{1,0:T(8,128)(2,1)S(1)}, bf16[256,2048]{1,0:T(8,128)(2,1)}, u32[]{:S(2)}) copy-start(bf16[256,2048]{1,0:T(8,128)(2,1)} %param.12) | copy-start | bytes 3145732
  206.4 6.2 %copy-start.5 = (f32[2048]{0:T(1024)S(1)}, f32[2048]{0:T(1024)}, u32[]{:S(2)}) copy-start(f32[2048]{0:T(1024)} %param.13) | copy-start | bytes 24580
  220.4 11.3 %copy-start.1 = (bf16[256,2048]{1,0:T(8,128)(2,1)S(1)}, bf16[256,2048]{1,0:T(8,128)(2,1)}, u32[]{:S(2)}) copy-start(bf16[256,2048]{1,0:T(8,128)(2,1)} %param.7) | copy-start | bytes 3145732
Sparse Core Ops, SparseCore 0:
  206.5 10.5 reduce-scatter.1
where the time goes:
time: 240 us; the launch traced here: 239 us
  starting transfers between devices  89.2 us (37%)
  waiting for transfers between devices  46.9 us (20%)
  matrix products  39.8 us (17%)
  local copies, waits for them, and re-layouts  26.9 us (11%)
  blocking collectives  16.8 us (7%)
  between operations  14.4 us (6%)
  other arithmetic  4.56 us (2%)
    ppermute x8, starting transfers between devices, from_behind(): return lax.ppermute(block, axis, route)  89.1 us
    ppermute x8, waiting for transfers between devices, from_behind(): return lax.ppermute(block, axis, route)  44.2 us
    unnamed x29, local copies, waits for them, and re-layouts  15.8 us
    dot_general x1, matrix products, attend(): jnp.einsum('hqk,khd->qhd', weights, value_group, preferred_element_type=j...  12 us
    dot_general x1, matrix products, shards(): jnp.dot(attended, out_weight, preferred_element_type=jnp.float32)  11.7 us
    sub x1, matrix products, attend(): exponent = jnp.exp(scores - largest)  8.2 us
    dot_general x1, matrix products, attend(): jnp.einsum('qhd,khd->hqk', query_group, key_group, preferred_element_type...  7.91 us
    concatenate x2, local copies, waits for them, and re-layouts, shards(): jnp.concatenate([couple[1] for couple in ordered] + [value_rows], 0)  7.78 us
  transfers between devices with their start and end apart: 9, of which 5 were waited for; matrix products, arithmetic and copies ran while one was open for 13% of the time, Pallas kernels for 0%

commit v1 on v0

v1 whole, which is shorter than its diff:
```python
import functools
import math

import jax
import jax.numpy as jnp
from jax import lax
from jax.experimental import pallas as pl
from jax.experimental.pallas import tpu as pltpu
from jax.sharding import PartitionSpec as P

HEAD_DIM = 128
BLOCK = 128
WINDOW_BLOCKS = 8
GROUP = 4
FAR = 5
MESH = pl.DeviceIdType.MESH
HIDE = -1e30


def kernel(
    q_hbm, k_hbm, v_hbm, pattern, w_hbm, h_hbm, gain,
    stream_ref, normed_ref,
    kv, qbuf, wbuf, hbuf, bias, acc, mixed, outgoing, incoming, square_out, square_in,
    own_sem, load_sem, send_sem, recv_sem, part_send, part_recv, sq_sem,
):
    rows, width = q_hbm.shape
    model = w_hbm.shape[1]
    subs = own_sem.shape[1]
    step_cols = width // subs
    piece = step_cols // 2
    shard = lax.axis_index("seq")
    section = lax.axis_index("section")
    count = lax.axis_size("seq")
    role = lax.rem(shard, GROUP)
    has_prev = shard >= GROUP
    has_next = shard + GROUP < count
    partner = 1 - section

    def base(off):
        return (FAR - off) * rows

    def view(off, k, part, tail):
        start = k * step_cols + (piece if part == 1 else 0)
        size = step_cols if part is None else piece
        cols = pl.ds(pl.multiple_of(start, piece), size)
        first, extent = (base(off) + rows - BLOCK, BLOCK) if tail else (base(off), rows)
        return kv.at[:, pl.ds(first, extent), cols]

    def part_index(part):
        return 1 if part == 1 else 0

    def send(index, k, off, target, to_off, part=None, tail=False):
        return pltpu.make_async_remote_copy(
            src_ref=view(off, k, part, tail),
            dst_ref=view(to_off, k, part, tail),
            send_sem=send_sem.at[index, k],
            recv_sem=recv_sem.at[to_off + 1, part_index(part), k],
            device_id={"seq": target},
            device_id_type=MESH,
        )

    def arrive(k, off, part=None, tail=False):
        pltpu.make_async_remote_copy(
            src_ref=view(off, k, part, tail),
            dst_ref=view(off, k, part, tail),
            send_sem=send_sem.at[0, k],
            recv_sem=recv_sem.at[off + 1, part_index(part), k],
            device_id={"section": partner},
            device_id_type=MESH,
        ).wait_recv()

    def own_loads(k):
        cols = pl.ds(pl.multiple_of(k * step_cols, step_cols), step_cols)
        return [
            pltpu.make_async_copy(
                source.at[:, cols], kv.at[i, pl.ds(base(0), rows), cols], own_sem.at[i, k]
            )
            for i, source in enumerate((k_hbm, v_hbm))
        ]

    a_own = [
        (0, 0, 1, 1, None, False, None),
        (1, 0, 2, 2, None, False, None),
        (2, 0, 4, 4, None, True, "next"),
    ]
    a_first = [(3, -1, 2, 1, 0, False, None), (4, -1, 4, 3, 0, False, "next")]
    a_second = [(5, 2, 1, 3, 0, False, "prev")]
    b_own = [
        (0, 0, -1, -1, 0, False, None),
        (1, 0, 2, 2, None, False, None),
        (2, 0, 4, 4, 1, False, "next"),
        (3, 0, 4, 4, 0, True, "next"),
    ]
    b_first = [(4, 1, 2, 3, 0, False, None), (5, 4, -1, 3, 1, False, "prev")]
    b_second = [(6, 2, -1, 1, 0, False, "prev")]
    c_own = [(0, 0, 1, 1, None, False, None), (1, 0, 4, 4, None, False, "next")]
    c_first = [(2, 2, 1, 3, 1, False, None), (3, 4, -2, 2, None, False, "prev")]
    c_second = [(4, 3, -2, 1, 1, False, "prev")]
    d_own = [(0, 0, 4, 4, None, False, "next")]
    d_first = [
        (1, 4, -2, 2, None, False, "prev"),
        (2, 4, -1, 3, None, False, "prev"),
        (3, 2, -1, 1, 1, False, None),
        (4, 1, 4, 5, 1, False, "next"),
    ]
    d_second = [(5, 5, -2, 3, 1, False, "prev")]
    table = [
        (a_own, [(-1, 0, False, None)], a_first,
         [(2, None, False, "prev")], a_second,
         [(1, 0, False, "prev"), (1, 1, False, "prev"), (3, 0, False, "prev"),
          (3, 1, False, "prev"), (4, None, True, "prev")]),
        (b_own, [(1, None, False, None), (4, 1, False, "prev")], b_first,
         [(2, None, False, "prev")], b_second,
         [(3, 0, False, "prev"), (3, 1, False, "prev"), (4, 0, True, "prev")]),
        (c_own, [(2, None, False, None), (4, None, False, "prev")], c_first,
         [(3, None, False, "prev")], c_second,
         [(1, 0, False, None), (1, 1, False, None)]),
        (d_own, [(4, None, False, "prev"), (2, None, False, None), (1, None, False, None)], d_first,
         [(5, 1, False, "prev")], d_second,
         [(3, 0, False, None), (3, 1, False, None)]),
    ]

    def grouped(entries, act):
        for need in (None, "prev", "next"):
            chosen = [e for e in entries if e[-1] == need]
            if not chosen:
                continue
            if need is None:
                for e in chosen:
                    act(e)
            else:
                @pl.when(has_prev if need == "prev" else has_next)
                def _():
                    for e in chosen:
                        act(e)

    def start_sends(entries, k):
        def act(e):
            index, off, step, to_off, part, tail, _ = e
            send(index, k, off, shard + step, to_off, part, tail).start()

        grouped(entries, act)

    def end_sends(entries, k):
        def act(e):
            index, off, step, to_off, part, tail, _ = e
            send(index, k, off, shard + step, to_off, part, tail).wait_send()

        grouped(entries, act)

    def waits(entries, k):
        grouped(entries, lambda e: arrive(k, e[0], e[1], e[2]))

    def by_role(body):
        for r in range(GROUP):
            @pl.when(role == r)
            def _():
                body(table[r])

    def first_sends(k):
        for copy in own_loads(k):
            copy.wait()
        by_role(lambda row: start_sends(row[0], k))

    def first_relay(k):
        def body(row):
            waits(row[1], k)
            start_sends(row[2], k)

        by_role(body)

    def second_relay(k):
        def body(row):
            waits(row[3], k)
            start_sends(row[4], k)

        by_role(body)

    q_load = pltpu.make_async_copy(q_hbm, qbuf, load_sem.at[0])
    w_load = pltpu.make_async_copy(w_hbm, wbuf, load_sem.at[1])
    h_load = pltpu.make_async_copy(h_hbm, hbuf, load_sem.at[2])

    for k in range(subs):
        for copy in own_loads(k):
            copy.start()
    q_load.start()
    w_load.start()
    h_load.start()

    barrier = pltpu.get_barrier_semaphore()
    across = jnp.where(lax.rem(role, 2) == 0, shard + 1, shard - 1)
    along = jnp.where(role < 2, shard + 2, shard - 2)
    pl.semaphore_signal(barrier, inc=1, device_id={"seq": across}, device_id_type=MESH)
    pl.semaphore_signal(barrier, inc=1, device_id={"seq": along}, device_id_type=MESH)
    pl.semaphore_signal(barrier, inc=1, device_id={"section": partner}, device_id_type=MESH)

    @pl.when(has_prev)
    def _():
        pl.semaphore_signal(
            barrier, inc=1, device_id={"seq": shard - GROUP}, device_id_type=MESH
        )

    @pl.when(has_next)
    def _():
        pl.semaphore_signal(
            barrier, inc=1, device_id={"seq": shard + GROUP}, device_id_type=MESH
        )

    pl.semaphore_wait(barrier, 3 + has_prev.astype(jnp.int32) + has_next.astype(jnp.int32))

    first_sends(0)

    for off in range(1, GROUP + 1):
        @pl.when(shard < off)
        def _():
            kv[:, pl.ds(base(off), rows), :] = jnp.zeros((2, rows, width), kv.dtype)

    query_place = lax.broadcasted_iota(jnp.int32, (BLOCK, BLOCK), 0)
    key_place = lax.broadcasted_iota(jnp.int32, (BLOCK, BLOCK), 1)
    blocks = rows // BLOCK
    span_blocks = WINDOW_BLOCKS - 1 + blocks
    for i in range(blocks):
        for g in range(span_blocks):
            j = i + WINDOW_BLOCKS - 1 - g
            if j < 0 or j >= WINDOW_BLOCKS:
                value = jnp.full((BLOCK, BLOCK), HIDE, jnp.float32)
            else:
                seen = (pattern[i, j] == 1) & (shard * blocks + i - j >= 0)
                level = jnp.where(seen, 0.0, HIDE).astype(jnp.float32)
                value = jnp.full((BLOCK, BLOCK), level, jnp.float32)
                if j == 0:
                    value = jnp.where(key_place <= query_place, value, HIDE)
            bias[i * BLOCK : (i + 1) * BLOCK, g * BLOCK : (g + 1) * BLOCK] = value
    acc[...] = jnp.zeros(acc.shape, acc.dtype)
    q_load.wait()
    w_load.wait()
    h_load.wait()

    key_first = base(GROUP) + rows - BLOCK
    key_span = span_blocks * BLOCK
    factor = math.log2(math.e) / math.sqrt(HEAD_DIM)
    tile = math.gcd(model, 1024)

    def attend(k):
        by_role(lambda row: waits(row[5], k))
        for n in range(step_cols // HEAD_DIM):
            cols = pl.ds(pl.multiple_of(k * step_cols + n * HEAD_DIM, HEAD_DIM), HEAD_DIM)
            query = qbuf[:, cols]
            keys = kv[0, pl.ds(key_first, key_span), cols]
            values = kv[1, pl.ds(key_first, key_span), cols]
            scores = lax.dot_general(
                query, keys, (((1,), (1,)), ((), ())), preferred_element_type=jnp.float32
            )
            scores = scores + bias[...]
            largest = jnp.max(scores, axis=1, keepdims=True)
            exponent = jnp.exp2((scores - largest) * factor)
            total = jnp.sum(exponent, axis=1, keepdims=True)
            mixture = jnp.dot(
                exponent.astype(jnp.bfloat16), values, preferred_element_type=jnp.float32
            )
            mixed[:, n * HEAD_DIM : (n + 1) * HEAD_DIM] = (mixture / total).astype(jnp.bfloat16)
        depth = pl.ds(pl.multiple_of(k * step_cols, step_cols), step_cols)
        for c in range(0, model, tile):
            acc[:, c : c + tile] += jnp.dot(
                mixed[...], wbuf[depth, c : c + tile], preferred_element_type=jnp.float32
            )

    @pl.loop(0, subs + 2)
    def _(t):
        @pl.when(t + 1 < subs)
        def _():
            first_sends(t + 1)

        @pl.when(t < subs)
        def _():
            first_relay(t)

        @pl.when((t >= 1) & (t - 1 < subs))
        def _():
            second_relay(t - 1)

        @pl.when(t >= 2)
        def _():
            attend(t - 2)

    pieces = part_send.shape[0]
    part_cols = width // pieces

    def part_copy(c):
        cols = pl.ds(c * part_cols, part_cols)
        return pltpu.make_async_remote_copy(
            src_ref=outgoing.at[:, cols],
            dst_ref=incoming.at[:, cols],
            send_sem=part_send.at[c],
            recv_sem=part_recv.at[c],
            device_id={"section": partner},
            device_id_type=MESH,
        )

    for c in range(pieces):
        start = pl.multiple_of(partner * width + c * part_cols, part_cols)
        outgoing[:, c * part_cols : (c + 1) * part_cols] = acc[:, pl.ds(start, part_cols)].astype(
            outgoing.dtype
        )
        if c >= 1:
            part_copy(c - 1).start()
    part_copy(pieces - 1).start()

    @pl.loop(0, subs)
    def _(k):
        def body(row):
            for entries in (row[0], row[2], row[4]):
                end_sends(entries, k)

        by_role(body)

    strip = 16
    mine = pl.multiple_of(section * width, part_cols)
    for c in range(pieces):
        part_copy(c).wait_recv()

    @pl.loop(0, rows // strip)
    def _(i):
        place = pl.ds(pl.multiple_of(i * strip, strip), strip)
        here = acc[place, pl.ds(mine, width)].astype(jnp.bfloat16).astype(jnp.float32)
        there = incoming[place, :].astype(jnp.float32)
        stream = hbuf[place, :].astype(jnp.float32) + (here + there)
        acc[place, pl.ds(mine, width)] = stream
        stream_ref[place, :] = stream.astype(stream_ref.dtype)
        squares = stream * stream
        lanes = squares[:, 0:128]
        for c in range(128, width, 128):
            lanes = lanes + squares[:, c : c + 128]
        square_out[place, :] = lanes

    square_copy = pltpu.make_async_remote_copy(
        src_ref=square_out,
        dst_ref=square_in,
        send_sem=sq_sem.at[0],
        recv_sem=sq_sem.at[1],
        device_id={"section": partner},
        device_id_type=MESH,
    )
    square_copy.start()
    for c in range(pieces):
        part_copy(c).wait_send()
    square_copy.wait()

    @pl.loop(0, rows // strip)
    def _(i):
        place = pl.ds(pl.multiple_of(i * strip, strip), strip)
        squares = jnp.sum(square_out[place, :] + square_in[place, :], axis=1, keepdims=True)
        inverse = lax.rsqrt(squares / model + 1e-06)
        stream = acc[place, pl.ds(mine, width)]
        normed_ref[place, :] = (stream * inverse * gain[...]).astype(normed_ref.dtype)


def shards(queries, key_rows, value_rows, block_pattern, out_weight, hidden, norm_gain):
    rows, width = queries.shape
    model = out_weight.shape[1]
    subs = width // (2 * HEAD_DIM)
    pieces = 4
    span = (WINDOW_BLOCKS - 1) * BLOCK + rows
    anywhere = pl.BlockSpec(memory_space=pl.ANY)
    vmem = pl.BlockSpec(memory_space=pltpu.VMEM)
    out = jax.ShapeDtypeStruct((rows, width), jnp.bfloat16)
    return pl.pallas_call(
        kernel,
        out_shape=(out, out),
        in_specs=[
            anywhere, anywhere, anywhere,
            pl.BlockSpec(memory_space=pltpu.SMEM),
            anywhere, anywhere, vmem,
        ],
        out_specs=(vmem, vmem),
        scratch_shapes=[
            pltpu.VMEM((2, (FAR + 2) * rows, width), jnp.bfloat16),
            pltpu.VMEM((rows, width), jnp.bfloat16),
            pltpu.VMEM((width, model), jnp.bfloat16),
            pltpu.VMEM((rows, width), jnp.bfloat16),
            pltpu.VMEM((rows, span), jnp.float32),
            pltpu.VMEM((rows, model), jnp.float32),
            pltpu.VMEM((rows, 2 * HEAD_DIM), jnp.bfloat16),
            pltpu.VMEM((rows, width), jnp.bfloat16),
            pltpu.VMEM((rows, width), jnp.bfloat16),
            pltpu.VMEM((rows, 128), jnp.float32),
            pltpu.VMEM((rows, 128), jnp.float32),
            pltpu.SemaphoreType.DMA((2, subs)),
            pltpu.SemaphoreType.DMA((3,)),
            pltpu.SemaphoreType.DMA((7, subs)),
            pltpu.SemaphoreType.DMA((FAR + 2, 2, subs)),
            pltpu.SemaphoreType.DMA((pieces,)),
            pltpu.SemaphoreType.DMA((pieces,)),
            pltpu.SemaphoreType.DMA((2,)),
        ],
        compiler_params=pltpu.CompilerParams(
            collective_id=0, has_side_effects=True, vmem_limit_bytes=62 * 1024 * 1024
        ),
    )(queries, key_rows, value_rows, block_pattern, out_weight, hidden, norm_gain[None, :])


def solution(mesh):
    placed = (
        P("seq", "section"),
        P("seq", "section"),
        P("seq", "section"),
        P("seq", None),
        P("section", None),
        P("seq", "section"),
        P("section"),
    )
    return jax.shard_map(
        shards,
        mesh=mesh,
        in_specs=placed,
        out_specs=(P("seq", "section"), P("seq", "section")),
        check_vma=False,
    )
```

time: 240 us -> 98.9 us (0.41)
  Pallas kernels: 0 us -> 93.4 us
  starting transfers between devices: 89.2 us -> 0 us
  waiting for transfers between devices: 46.9 us -> 0 us
  matrix products: 39.8 us -> 0 us
  local copies, waits for them, and re-layouts: 26.9 us -> 4.61 us
  blocking collectives: 16.8 us -> 0 us
  between operations: 14.4 us -> 0.64 us
  other arithmetic: 4.56 us -> 0 us
    pallas_call x0 -> x1, Pallas kernels: none -> 93.4 us  [shards(): pl.pallas_call(kernel, out_shape=(out, out), in_specs=[anywhere, anywhere...]
    ppermute x8 -> x0, starting transfers between devices: 89.1 us -> none  [from_behind(): return lax.ppermute(block, axis, route)]
    ppermute x8 -> x0, waiting for transfers between devices: 44.2 us -> none  [from_behind(): return lax.ppermute(block, axis, route)]
    dot_general x3 -> x0, matrix products: 31.6 us -> none  [the longest x1 12 us: attend(): jnp.einsum('hqk,khd->qhd', weights, value_group, preferred_element_type=j...]
    all_to_all x3 -> x0, blocking collectives: 15 us -> none  [the longest x1 5.73 us: shards(): lax.all_to_all(hidden, 'section', split_axis=0, concat_axis=1, tiled=True)]
    unnamed x29 -> x2, local copies, waits for them, and re-layouts: 15.8 us -> 4.61 us
    sub x1 -> x0, matrix products: 8.2 us -> none  [attend(): exponent = jnp.exp(scores - largest)]
    concatenate x3 -> x0, local copies, waits for them, and re-layouts: 7.85 us -> none  [the longest x2 7.78 us: shards(): jnp.concatenate([couple[1] for couple in ordered] + [value_rows], 0)]
  transfers between devices with their start and end apart: 9 -> 0, of which waited for: 5 -> 0; matrix products, arithmetic and copies ran while one was open for 13% -> 0% of each run, Pallas kernels for 0% -> 0%
where the time goes in v1:
time: 98.9 us; the launch traced here: 98.7 us
  Pallas kernels  93.4 us (94%)
  local copies, waits for them, and re-layouts  4.61 us (5%)
    pallas_call x1, Pallas kernels, shards(): pl.pallas_call(kernel, out_shape=(out, out), in_specs=[anywhere, anywhere...  93.4 us
    unnamed x2, local copies, waits for them, and re-layouts  4.61 us

profile of v1, /device:TPU:9, one launch (start us, length us, event | category | flops | bytes accessed | tf_op | source)
XLA Modules:
  0.0 98.7 jit_solution(4885763684045387540)
XLA Ops:
  0.6 93.4 %shard_map.86 = (bf16[256,2048]{1,0:T(8,128)(2,1)}, bf16[256,2048]{1,0:T(8,128)(2,1)}) custom-call(bf16[256,2048]{1,0:T(8,128)(2,1)} %q_hbm.1, bf16[256,2048]{1,0:T(8,128)(2,1)} %k_hbm.1, bf16[256,2048]{1,0:T(8,128)(2,1)} %v_hbm.1, s32[2,8]{1,0:T(2,128)} %pattern.1, bf16[2048,4096]{1,0:T(8,128)(2,1)} %w_hbm.1, bf16[256,2048]{1,0:T(8,128)(2,1)} %h_hbm.1, ...), custom_call_target="tpu_custom_call" | custom-call | tf_op jit(solution)/shard_map/pallas_call | solution.py:367
  94.1 2.3 %copy.11 = bf16[256,2048]{1,0:T(8,128)(2,1)} copy(bf16[256,2048]{1,0:T(8,128)(2,1)} %get-tuple-element.4) | data formatting | bytes 2097152
  96.4 2.3 %copy.12 = bf16[256,2048]{1,0:T(8,128)(2,1)} copy(bf16[256,2048]{1,0:T(8,128)(2,1)} %get-tuple-element.5) | data formatting | bytes 2097152

commit v2 on v1

--- a/solution.py
+++ b/solution.py
@@ -18,9 +18,9 @@
 
 
 def kernel(
-    q_hbm, k_hbm, v_hbm, pattern, w_hbm, h_hbm, gain,
-    stream_ref, normed_ref,
-    kv, qbuf, wbuf, hbuf, bias, acc, mixed, outgoing, incoming, square_out, square_in,
+    q_hbm, k_hbm, v_hbm, pattern, w_hbm, h_hbm,
+    stream_ref, square_ref,
+    kv, qbuf, wbuf, hbuf, bias, acc, mixed, mine, outgoing, incoming, square_out, square_in,
     own_sem, load_sem, send_sem, recv_sem, part_send, part_recv, sq_sem,
 ):
     rows, width = q_hbm.shape
@@ -78,46 +78,49 @@
             for i, source in enumerate((k_hbm, v_hbm))
         ]
 
-    a_own = [
-        (0, 0, 1, 1, None, False, None),
-        (1, 0, 2, 2, None, False, None),
-        (2, 0, 4, 4, None, True, "next"),
-    ]
-    a_first = [(3, -1, 2, 1, 0, False, None), (4, -1, 4, 3, 0, False, "next")]
-    a_second = [(5, 2, 1, 3, 0, False, "prev")]
-    b_own = [
-        (0, 0, -1, -1, 0, False, None),
-        (1, 0, 2, 2, None, False, None),
-        (2, 0, 4, 4, 1, False, "next"),
-        (3, 0, 4, 4, 0, True, "next"),
-    ]
-    b_first = [(4, 1, 2, 3, 0, False, None), (5, 4, -1, 3, 1, False, "prev")]
-    b_second = [(6, 2, -1, 1, 0, False, "prev")]
-    c_own = [(0, 0, 1, 1, None, False, None), (1, 0, 4, 4, None, False, "next")]
-    c_first = [(2, 2, 1, 3, 1, False, None), (3, 4, -2, 2, None, False, "prev")]
-    c_second = [(4, 3, -2, 1, 1, False, "prev")]
-    d_own = [(0, 0, 4, 4, None, False, "next")]
-    d_first = [
-        (1, 4, -2, 2, None, False, "prev"),
-        (2, 4, -1, 3, None, False, "prev"),
-        (3, 2, -1, 1, 1, False, None),
-        (4, 1, 4, 5, 1, False, "next"),
-    ]
-    d_second = [(5, 5, -2, 3, 1, False, "prev")]
     table = [
-        (a_own, [(-1, 0, False, None)], a_first,
-         [(2, None, False, "prev")], a_second,
-         [(1, 0, False, "prev"), (1, 1, False, "prev"), (3, 0, False, "prev"),
-          (3, 1, False, "prev"), (4, None, True, "prev")]),
-        (b_own, [(1, None, False, None), (4, 1, False, "prev")], b_first,
-         [(2, None, False, "prev")], b_second,
-         [(3, 0, False, "prev"), (3, 1, False, "prev"), (4, 0, True, "prev")]),
-        (c_own, [(2, None, False, None), (4, None, False, "prev")], c_first,
-         [(3, None, False, "prev")], c_second,
-         [(1, 0, False, None), (1, 1, False, None)]),
-        (d_own, [(4, None, False, "prev"), (2, None, False, None), (1, None, False, None)], d_first,
-         [(5, 1, False, "prev")], d_second,
-         [(3, 0, False, None), (3, 1, False, None)]),
+        (
+            [(0, 0, 1, 1, 0, False, None), (1, 0, 2, 2, 0, False, None),
+             (2, 0, 1, 1, 1, False, None), (3, 0, 2, 2, 1, False, None),
+             (4, 0, 4, 4, None, True, "next")],
+            [([(-1, 0, False, None)],
+              [(5, -1, 2, 1, 0, False, None), (6, -1, 4, 3, 0, False, "next")])],
+            [([(2, 0, False, "prev")], [(7, 2, 1, 3, 0, False, "prev")])],
+            [(2, 1, False, "prev"), (3, 0, False, "prev"), (4, None, True, "prev"),
+             (3, 1, False, "prev"), (1, 0, False, "prev"), (1, 1, False, "prev")],
+        ),
+        (
+            [(0, 0, -1, -1, 0, False, None), (1, 0, 2, 2, 1, False, None),
+             (2, 0, 4, 4, 1, False, "next"), (3, 0, 2, 2, 0, False, None),
+             (4, 0, 4, 4, 0, True, "next")],
+            [([(4, 1, False, "prev")], [(5, 4, -1, 3, 1, False, "prev")]),
+             ([(1, 0, False, None)], [(6, 1, 2, 3, 0, False, None)])],
+            [([(2, 0, False, "prev")], [(7, 2, -1, 1, 0, False, "prev")])],
+            [(1, 1, False, None), (2, 1, False, "prev"), (4, 0, True, "prev"),
+             (3, 0, False, "prev"), (3, 1, False, "prev")],
+        ),
+        (
+            [(0, 0, 4, 4, 0, False, "next"), (1, 0, 1, 1, 1, False, None),
+             (2, 0, 4, 4, 1, False, "next"), (3, 0, 1, 1, 0, False, None)],
+            [([(4, 0, False, "prev")], [(4, 4, -2, 2, 0, False, "prev")]),
+             ([(4, 1, False, "prev")], [(5, 4, -2, 2, 1, False, "prev")]),
+             ([(2, 1, False, None)], [(6, 2, 1, 3, 1, False, None)])],
+            [([(3, 1, False, "prev")], [(7, 3, -2, 1, 1, False, "prev")])],
+            [(2, 0, False, None), (3, 0, False, "prev"),
+             (1, 0, False, None), (1, 1, False, None)],
+        ),
+        (
+            [(0, 0, 4, 4, 0, False, "next"), (1, 0, 4, 4, 1, False, "next")],
+            [([(4, 0, False, "prev")],
+              [(2, 4, -2, 2, 0, False, "prev"), (3, 4, -1, 3, 0, False, "prev")]),
+             ([(4, 1, False, "prev")],
+              [(4, 4, -1, 3, 1, False, "prev"), (5, 4, -2, 2, 1, False, "prev")]),
+             ([(2, 1, False, None)], [(6, 2, -1, 1, 1, False, None)]),
+             ([(1, 1, False, None)], [(7, 1, 4, 5, 1, False, "next")])],
+            [([(5, 1, False, "prev")], [(8, 5, -2, 3, 1, False, "prev")])],
+            [(2, 0, False, None), (1, 0, False, None),
+             (3, 0, False, None), (3, 1, False, None)],
+        ),
     ]
 
     def grouped(entries, act):
@@ -162,17 +165,11 @@
             copy.wait()
         by_role(lambda row: start_sends(row[0], k))
 
-    def first_relay(k):
+    def relay(which, k):
         def body(row):
-            waits(row[1], k)
-            start_sends(row[2], k)
-
-        by_role(body)
-
-    def second_relay(k):
-        def body(row):
-            waits(row[3], k)
-            start_sends(row[4], k)
+            for needed, sends in row[which]:
+                waits(needed, k)
+                start_sends(sends, k)
 
         by_role(body)
 
@@ -241,8 +238,8 @@
     factor = math.log2(math.e) / math.sqrt(HEAD_DIM)
     tile = math.gcd(model, 1024)
 
-    def attend(k):
-        by_role(lambda row: waits(row[5], k))
+    def heads(k):
+        by_role(lambda row: waits(row[3], k))
         for n in range(step_cols // HEAD_DIM):
             cols = pl.ds(pl.multiple_of(k * step_cols + n * HEAD_DIM, HEAD_DIM), HEAD_DIM)
             query = qbuf[:, cols]
@@ -259,29 +256,34 @@
                 exponent.astype(jnp.bfloat16), values, preferred_element_type=jnp.float32
             )
             mixed[:, n * HEAD_DIM : (n + 1) * HEAD_DIM] = (mixture / total).astype(jnp.bfloat16)
+
+    def attend(k):
+        heads(k)
         depth = pl.ds(pl.multiple_of(k * step_cols, step_cols), step_cols)
         for c in range(0, model, tile):
             acc[:, c : c + tile] += jnp.dot(
                 mixed[...], wbuf[depth, c : c + tile], preferred_element_type=jnp.float32
             )
 
-    @pl.loop(0, subs + 2)
+    @pl.loop(0, subs)
     def _(t):
         @pl.when(t + 1 < subs)
         def _():
             first_sends(t + 1)
 
-        @pl.when(t < subs)
+        relay(1, t)
+
+        @pl.when(t >= 1)
         def _():
-            first_relay(t)
-
-        @pl.when((t >= 1) & (t - 1 < subs))
-        def _():
-            second_relay(t - 1)
+            relay(2, t - 1)
 
         @pl.when(t >= 2)
         def _():
             attend(t - 2)
+
+    attend(subs - 2)
+    relay(2, subs - 1)
+    heads(subs - 1)
 
     pieces = part_send.shape[0]
     part_cols = width // pieces
@@ -297,36 +299,37 @@
             device_id_type=MESH,
         )
 
+    last = pl.ds((subs - 1) * step_cols, step_cols)
+
+    def last_sum(start):
+        cols = pl.ds(pl.multiple_of(start, part_cols), part_cols)
+        return acc[:, cols] + jnp.dot(
+            mixed[...], wbuf[last, cols], preferred_element_type=jnp.float32
+        )
+
     for c in range(pieces):
-        start = pl.multiple_of(partner * width + c * part_cols, part_cols)
-        outgoing[:, c * part_cols : (c + 1) * part_cols] = acc[:, pl.ds(start, part_cols)].astype(
-            outgoing.dtype
-        )
+        outgoing[:, c * part_cols : (c + 1) * part_cols] = last_sum(
+            partner * width + c * part_cols
+        ).astype(outgoing.dtype)
         if c >= 1:
             part_copy(c - 1).start()
-    part_copy(pieces - 1).start()
-
-    @pl.loop(0, subs)
-    def _(k):
-        def body(row):
-            for entries in (row[0], row[2], row[4]):
-                end_sends(entries, k)
-
-        by_role(body)
-
-    strip = 16
-    mine = pl.multiple_of(section * width, part_cols)
+    for c in range(pieces):
+        cols = slice(c * part_cols, (c + 1) * part_cols)
+        mine[:, cols] = last_sum(section * width + c * part_cols).astype(mine.dtype)
+        if c == 0:
+            part_copy(pieces - 1).start()
     for c in range(pieces):
         part_copy(c).wait_recv()
+
+    strip = 16
 
     @pl.loop(0, rows // strip)
     def _(i):
         place = pl.ds(pl.multiple_of(i * strip, strip), strip)
-        here = acc[place, pl.ds(mine, width)].astype(jnp.bfloat16).astype(jnp.float32)
+        here = mine[place, :].astype(jnp.float32)
         there = incoming[place, :].astype(jnp.float32)
         stream = hbuf[place, :].astype(jnp.float32) + (here + there)
-        acc[place, pl.ds(mine, width)] = stream
-        stream_ref[place, :] = stream.astype(stream_ref.dtype)
+        stream_ref[place, :] = stream
         squares = stream * stream
         lanes = squares[:, 0:128]
         for c in range(128, width, 128):
@@ -342,17 +345,21 @@
         device_id_type=MESH,
     )
     square_copy.start()
+
+    @pl.loop(0, subs)
+    def _(k):
+        def body(row):
+            end_sends(row[0], k)
+            for which in (1, 2):
+                for _, sends in row[which]:
+                    end_sends(sends, k)
+
+        by_role(body)
+
     for c in range(pieces):
         part_copy(c).wait_send()
     square_copy.wait()
-
-    @pl.loop(0, rows // strip)
-    def _(i):
-        place = pl.ds(pl.multiple_of(i * strip, strip), strip)
-        squares = jnp.sum(square_out[place, :] + square_in[place, :], axis=1, keepdims=True)
-        inverse = lax.rsqrt(squares / model + 1e-06)
-        stream = acc[place, pl.ds(mine, width)]
-        normed_ref[place, :] = (stream * inverse * gain[...]).astype(normed_ref.dtype)
+    square_ref[...] = square_out[...] + square_in[...]
 
 
 def shards(queries, key_rows, value_rows, block_pattern, out_weight, hidden, norm_gain):
@@ -363,14 +370,16 @@
     span = (WINDOW_BLOCKS - 1) * BLOCK + rows
     anywhere = pl.BlockSpec(memory_space=pl.ANY)
     vmem = pl.BlockSpec(memory_space=pltpu.VMEM)
-    out = jax.ShapeDtypeStruct((rows, width), jnp.bfloat16)
-    return pl.pallas_call(
+    stream, squares = pl.pallas_call(
         kernel,
-        out_shape=(out, out),
+        out_shape=(
+            jax.ShapeDtypeStruct((rows, width), jnp.float32),
+            jax.ShapeDtypeStruct((rows, 128), jnp.float32),
+        ),
         in_specs=[
             anywhere, anywhere, anywhere,
             pl.BlockSpec(memory_space=pltpu.SMEM),
-            anywhere, anywhere, vmem,
+            anywhere, anywhere,
         ],
         out_specs=(vmem, vmem),
         scratch_shapes=[
@@ -383,11 +392,12 @@
             pltpu.VMEM((rows, 2 * HEAD_DIM), jnp.bfloat16),
             pltpu.VMEM((rows, width), jnp.bfloat16),
             pltpu.VMEM((rows, width), jnp.bfloat16),
+            pltpu.VMEM((rows, width), jnp.bfloat16),
             pltpu.VMEM((rows, 128), jnp.float32),
             pltpu.VMEM((rows, 128), jnp.float32),
             pltpu.SemaphoreType.DMA((2, subs)),
             pltpu.SemaphoreType.DMA((3,)),
-            pltpu.SemaphoreType.DMA((7, subs)),
+            pltpu.SemaphoreType.DMA((9, subs)),
             pltpu.SemaphoreType.DMA((FAR + 2, 2, subs)),
             pltpu.SemaphoreType.DMA((pieces,)),
             pltpu.SemaphoreType.DMA((pieces,)),
@@ -396,7 +406,10 @@
         compiler_params=pltpu.CompilerParams(
             collective_id=0, has_side_effects=True, vmem_limit_bytes=62 * 1024 * 1024
         ),
-    )(queries, key_rows, value_rows, block_pattern, out_weight, hidden, norm_gain[None, :])
+    )(queries, key_rows, value_rows, block_pattern, out_weight, hidden)
+    mean_square = jnp.sum(squares, axis=1, keepdims=True) / model
+    normed = stream * lax.rsqrt(mean_square + 1e-06) * norm_gain[None, :]
+    return (stream.astype(jnp.bfloat16), normed.astype(jnp.bfloat16))
 
 
 def solution(mesh):

time: 98.9 us -> 97 us (0.981)
  other arithmetic: 0 us -> 4.8 us
  local copies, waits for them, and re-layouts: 4.61 us -> 0.01 us
  Pallas kernels: 93.4 us -> 91.3 us
    unnamed x2, local copies, waits for them, and re-layouts: 4.61 us -> 0.01 us
    convert_element_type x0 -> x1, other arithmetic: none -> 3.78 us  [shards(): return (stream.astype(jnp.bfloat16), normed.astype(jnp.bfloat16))]
    pallas_call x1, Pallas kernels: 93.4 us -> 91.3 us  [shards(): pl.pallas_call(kernel, out_shape=(jax.ShapeDtypeStruct((rows, width), jnp...]
    reduce_sum x0 -> x1, other arithmetic: none -> 1.02 us  [shards(): mean_square = jnp.sum(squares, axis=1, keepdims=True) / model]
where the time goes in v2:
time: 97 us; the launch traced here: 96.8 us
  Pallas kernels  91.3 us (94%)
  other arithmetic  4.8 us (5%)
    pallas_call x1, Pallas kernels, shards(): pl.pallas_call(kernel, out_shape=(jax.ShapeDtypeStruct((rows, width), jnp...  91.3 us
    convert_element_type x1, other arithmetic, shards(): return (stream.astype(jnp.bfloat16), normed.astype(jnp.bfloat16))  3.78 us

profile of v2, /device:TPU:9, one launch (start us, length us, event | category | flops | bytes accessed | tf_op | source)
XLA Modules:
  0.0 96.8 jit_solution(17815816309814939362)
XLA Ops:
  0.6 0.0 copy-start
  0.6 91.3 %shard_map.86 = (f32[256,2048]{1,0:T(8,128)}, f32[256,128]{1,0:T(8,128)}) custom-call(bf16[256,2048]{1,0:T(8,128)(2,1)} %q_hbm.1, bf16[256,2048]{1,0:T(8,128)(2,1)} %k_hbm.1, bf16[256,2048]{1,0:T(8,128)(2,1)} %v_hbm.1, s32[2,8]{1,0:T(2,128)} %pattern.1, bf16[2048,4096]{1,0:T(8,128)(2,1)} %w_hbm.1, bf16[256,2048]{1,0:T(8,128)(2,1)} %h_hbm.1), custom_call_target="tpu_custom_call" | custom-call | tf_op jit(solution)/shard_map/pallas_call | solution.py:373
  92.0 1.0 %reduce_sum.9 = f32[256]{0:T(256)S(1)} reduce(f32[256,128]{1,0:T(8,128)} %get-tuple-element.5, f32[]{:T(128)} %constant.1.clone.1), dimensions={1}, to_apply=%region_0.0 | reduce | flops 32512 | bytes 132100 | tf_op jit(solution)/shard_map/reduce_sum | solution.py:410
  93.0 0.0 copy-done
  93.0 3.8 %multiply_convert_fusion = (bf16[256,2048]{1,0:T(8,128)(2,1)}, bf16[256,2048]{1,0:T(8,128)(2,1)}) fusion(f32[256,2048]{1,0:T(8,128)} %get-tuple-element.4, f32[2048]{0:T(1024)S(1)} %copy-done, f32[256]{0:T(256)S(1)} %add_rsqrt_fusion), kind=kLoop, calls=%fused_computation | loop fusion | flops 2097152 | bytes 4203520 | tf_op jit(solution)/shard_map/convert_element_type | solution.py:412
  (1 shorter events, 0.0 us)
Async XLA Ops:
  0.6 92.4 %copy-start = (f32[2048]{0:T(1024)S(1)}, f32[2048]{0:T(1024)}, u32[]{:S(2)}) copy-start(f32[2048]{0:T(1024)} %param.13) | copy-start | bytes 24580

commit v3 on v2

--- a/solution.py
+++ b/solution.py
@@ -13,6 +13,7 @@
 WINDOW_BLOCKS = 8
 GROUP = 4
 FAR = 5
+NEAR = -2
 MESH = pl.DeviceIdType.MESH
 HIDE = -1e30
 
@@ -54,7 +55,7 @@
             src_ref=view(off, k, part, tail),
             dst_ref=view(to_off, k, part, tail),
             send_sem=send_sem.at[index, k],
-            recv_sem=recv_sem.at[to_off + 1, part_index(part), k],
+            recv_sem=recv_sem.at[to_off - NEAR, part_index(part), k],
             device_id={"seq": target},
             device_id_type=MESH,
         )
@@ -64,7 +65,7 @@
             src_ref=view(off, k, part, tail),
             dst_ref=view(off, k, part, tail),
             send_sem=send_sem.at[0, k],
-            recv_sem=recv_sem.at[off + 1, part_index(part), k],
+            recv_sem=recv_sem.at[off - NEAR, part_index(part), k],
             device_id={"section": partner},
             device_id_type=MESH,
         ).wait_recv()
@@ -80,12 +81,13 @@
 
     table = [
         (
-            [(0, 0, 1, 1, 0, False, None), (1, 0, 2, 2, 0, False, None),
-             (2, 0, 1, 1, 1, False, None), (3, 0, 2, 2, 1, False, None),
+            [(0, 0, 2, 2, 0, False, None), (1, 0, 1, 1, 0, False, None),
+             (2, 0, 2, 2, 1, False, None), (3, 0, 1, 1, 1, False, None),
              (4, 0, 4, 4, None, True, "next")],
             [([(-1, 0, False, None)],
-              [(5, -1, 2, 1, 0, False, None), (6, -1, 4, 3, 0, False, "next")])],
-            [([(2, 0, False, "prev")], [(7, 2, 1, 3, 0, False, "prev")])],
+              [(6, -1, 4, 3, 0, False, "next"), (5, -1, 2, 1, 0, False, None)]),
+             ([(-2, 0, False, "next")], [(7, -2, 4, 2, 0, False, "next")])],
+            [([(2, 0, False, "prev")], [(8, 2, 1, 3, 0, False, "prev")])],
             [(2, 1, False, "prev"), (3, 0, False, "prev"), (4, None, True, "prev"),
              (3, 1, False, "prev"), (1, 0, False, "prev"), (1, 1, False, "prev")],
         ),
@@ -94,29 +96,30 @@
              (2, 0, 4, 4, 1, False, "next"), (3, 0, 2, 2, 0, False, None),
              (4, 0, 4, 4, 0, True, "next")],
             [([(4, 1, False, "prev")], [(5, 4, -1, 3, 1, False, "prev")]),
+             ([(-2, 1, False, "next")], [(8, -2, 4, 2, 1, False, "next")]),
              ([(1, 0, False, None)], [(6, 1, 2, 3, 0, False, None)])],
             [([(2, 0, False, "prev")], [(7, 2, -1, 1, 0, False, "prev")])],
             [(1, 1, False, None), (2, 1, False, "prev"), (4, 0, True, "prev"),
              (3, 0, False, "prev"), (3, 1, False, "prev")],
         ),
         (
-            [(0, 0, 4, 4, 0, False, "next"), (1, 0, 1, 1, 1, False, None),
-             (2, 0, 4, 4, 1, False, "next"), (3, 0, 1, 1, 0, False, None)],
-            [([(4, 0, False, "prev")], [(4, 4, -2, 2, 0, False, "prev")]),
-             ([(4, 1, False, "prev")], [(5, 4, -2, 2, 1, False, "prev")]),
+            [(2, 0, 4, 4, 1, False, "next"), (0, 0, -2, -2, 0, False, "next"),
+             (1, 0, 1, 1, 1, False, None), (3, 0, 1, 1, 0, False, None),
+             (4, 0, 4, 4, 0, True, "next")],
+            [([(4, 1, False, "prev")], [(5, 4, -2, 2, 1, False, "prev")]),
+             ([(-1, 0, False, "next")], [(8, -1, 4, 3, 0, False, "next")]),
              ([(2, 1, False, None)], [(6, 2, 1, 3, 1, False, None)])],
             [([(3, 1, False, "prev")], [(7, 3, -2, 1, 1, False, "prev")])],
-            [(2, 0, False, None), (3, 0, False, "prev"),
+            [(2, 0, False, None), (3, 0, False, "prev"), (4, 0, True, "prev"),
              (1, 0, False, None), (1, 1, False, None)],
         ),
         (
-            [(0, 0, 4, 4, 0, False, "next"), (1, 0, 4, 4, 1, False, "next")],
-            [([(4, 0, False, "prev")],
-              [(2, 4, -2, 2, 0, False, "prev"), (3, 4, -1, 3, 0, False, "prev")]),
-             ([(4, 1, False, "prev")],
-              [(4, 4, -1, 3, 1, False, "prev"), (5, 4, -2, 2, 1, False, "prev")]),
-             ([(2, 1, False, None)], [(6, 2, -1, 1, 1, False, None)]),
-             ([(1, 1, False, None)], [(7, 1, 4, 5, 1, False, "next")])],
+            [(0, 0, 4, 4, 0, False, "next"), (2, 0, -2, -2, 1, False, "next"),
+             (3, 0, -1, -1, 0, False, "next"), (1, 0, 4, 4, 1, False, "next")],
+            [([(4, 0, False, "prev")], [(4, 4, -2, 2, 0, False, "prev")]),
+             ([(4, 1, False, "prev")], [(5, 4, -1, 3, 1, False, "prev")]),
+             ([(1, 1, False, None)], [(7, 1, 4, 5, 1, False, "next")]),
+             ([(2, 1, False, None)], [(6, 2, -1, 1, 1, False, None)])],
             [([(5, 1, False, "prev")], [(8, 5, -2, 3, 1, False, "prev")])],
             [(2, 0, False, None), (1, 0, False, None),
              (3, 0, False, None), (3, 1, False, None)],
@@ -383,7 +386,7 @@
         ],
         out_specs=(vmem, vmem),
         scratch_shapes=[
-            pltpu.VMEM((2, (FAR + 2) * rows, width), jnp.bfloat16),
+            pltpu.VMEM((2, (FAR + 1 - NEAR) * rows, width), jnp.bfloat16),
             pltpu.VMEM((rows, width), jnp.bfloat16),
             pltpu.VMEM((width, model), jnp.bfloat16),
             pltpu.VMEM((rows, width), jnp.bfloat16),
@@ -398,7 +401,7 @@
             pltpu.SemaphoreType.DMA((2, subs)),
             pltpu.SemaphoreType.DMA((3,)),
             pltpu.SemaphoreType.DMA((9, subs)),
-            pltpu.SemaphoreType.DMA((FAR + 2, 2, subs)),
+            pltpu.SemaphoreType.DMA((FAR + 1 - NEAR, 2, subs)),
             pltpu.SemaphoreType.DMA((pieces,)),
             pltpu.SemaphoreType.DMA((pieces,)),
             pltpu.SemaphoreType.DMA((2,)),

time: 97 us -> 95 us (0.979)
  Pallas kernels: 91.3 us -> 89.4 us
    pallas_call x1, Pallas kernels: 91.3 us -> 89.4 us  [shards(): pl.pallas_call(kernel, out_shape=(jax.ShapeDtypeStruct((rows, width), jnp...]
where the time goes in v3:
time: 95 us; the launch traced here: 94.8 us
  Pallas kernels  89.4 us (94%)
  other arithmetic  4.8 us (5%)
    pallas_call x1, Pallas kernels, shards(): pl.pallas_call(kernel, out_shape=(jax.ShapeDtypeStruct((rows, width), jnp...  89.4 us
    convert_element_type x1, other arithmetic, shards(): return (stream.astype(jnp.bfloat16), normed.astype(jnp.bfloat16))  3.78 us

profile of v3, /device:TPU:9, one launch (start us, length us, event | category | flops | bytes accessed | tf_op | source)
XLA Modules:
  0.0 94.8 jit_solution(14609400794678946331)
XLA Ops:
  0.6 0.0 copy-start
  0.6 89.4 %shard_map.86 = (f32[256,2048]{1,0:T(8,128)}, f32[256,128]{1,0:T(8,128)}) custom-call(bf16[256,2048]{1,0:T(8,128)(2,1)} %q_hbm.1, bf16[256,2048]{1,0:T(8,128)(2,1)} %k_hbm.1, bf16[256,2048]{1,0:T(8,128)(2,1)} %v_hbm.1, s32[2,8]{1,0:T(2,128)} %pattern.1, bf16[2048,4096]{1,0:T(8,128)(2,1)} %w_hbm.1, bf16[256,2048]{1,0:T(8,128)(2,1)} %h_hbm.1), custom_call_target="tpu_custom_call" | custom-call | tf_op jit(solution)/shard_map/pallas_call | solution.py:376
  90.0 1.0 %reduce_sum.9 = f32[256]{0:T(256)S(1)} reduce(f32[256,128]{1,0:T(8,128)} %get-tuple-element.5, f32[]{:T(128)} %constant.1.clone.1), dimensions={1}, to_apply=%region_0.0 | reduce | flops 32512 | bytes 132100 | tf_op jit(solution)/shard_map/reduce_sum | solution.py:413
  91.0 0.0 copy-done
  91.1 3.8 %multiply_convert_fusion = (bf16[256,2048]{1,0:T(8,128)(2,1)}, bf16[256,2048]{1,0:T(8,128)(2,1)}) fusion(f32[256,2048]{1,0:T(8,128)} %get-tuple-element.4, f32[2048]{0:T(1024)S(1)} %copy-done, f32[256]{0:T(256)S(1)} %add_rsqrt_fusion), kind=kLoop, calls=%fused_computation | loop fusion | flops 2097152 | bytes 4203520 | tf_op jit(solution)/shard_map/convert_element_type | solution.py:415
  (1 shorter events, 0.0 us)
Async XLA Ops:
  0.6 90.4 %copy-start = (f32[2048]{0:T(1024)S(1)}, f32[2048]{0:T(1024)}, u32[]{:S(2)}) copy-start(f32[2048]{0:T(1024)} %param.13) | copy-start | bytes 24580

commit v4 on v3

--- a/solution.py
+++ b/solution.py
@@ -280,12 +280,13 @@
         def _():
             relay(2, t - 1)
 
-        @pl.when(t >= 2)
+        @pl.when(t >= 3)
         def _():
-            attend(t - 2)
-
+            attend(t - 3)
+
+    attend(subs - 3)
+    relay(2, subs - 1)
     attend(subs - 2)
-    relay(2, subs - 1)
     heads(subs - 1)
 
     pieces = part_send.shape[0]

time: 95 us -> 92.7 us (0.976)
  Pallas kernels: 89.4 us -> 86.7 us
    pallas_call x1, Pallas kernels: 89.4 us -> 86.7 us  [shards(): pl.pallas_call(kernel, out_shape=(jax.ShapeDtypeStruct((rows, width), jnp...]
where the time goes in v4:
time: 92.7 us; the launch traced here: 92.1 us
  Pallas kernels  86.7 us (94%)
  other arithmetic  4.8 us (5%)
    pallas_call x1, Pallas kernels, shards(): pl.pallas_call(kernel, out_shape=(jax.ShapeDtypeStruct((rows, width), jnp...  86.7 us
    convert_element_type x1, other arithmetic, shards(): return (stream.astype(jnp.bfloat16), normed.astype(jnp.bfloat16))  3.78 us

profile of v4, /device:TPU:9, one launch (start us, length us, event | category | flops | bytes accessed | tf_op | source)
XLA Modules:
  0.0 92.1 jit_solution(18011184428929083007)
XLA Ops:
  0.6 0.0 copy-start
  0.6 86.7 %shard_map.86 = (f32[256,2048]{1,0:T(8,128)}, f32[256,128]{1,0:T(8,128)}) custom-call(bf16[256,2048]{1,0:T(8,128)(2,1)} %q_hbm.1, bf16[256,2048]{1,0:T(8,128)(2,1)} %k_hbm.1, bf16[256,2048]{1,0:T(8,128)(2,1)} %v_hbm.1, s32[2,8]{1,0:T(2,128)} %pattern.1, bf16[2048,4096]{1,0:T(8,128)(2,1)} %w_hbm.1, bf16[256,2048]{1,0:T(8,128)(2,1)} %h_hbm.1), custom_call_target="tpu_custom_call" | custom-call | tf_op jit(solution)/shard_map/pallas_call | solution.py:377
  87.3 1.0 %reduce_sum.9 = f32[256]{0:T(256)S(1)} reduce(f32[256,128]{1,0:T(8,128)} %get-tuple-element.5, f32[]{:T(128)} %constant.1.clone.1), dimensions={1}, to_apply=%region_0.0 | reduce | flops 32512 | bytes 132100 | tf_op jit(solution)/shard_map/reduce_sum | solution.py:414
  88.3 0.0 copy-done
  88.4 3.8 %multiply_convert_fusion = (bf16[256,2048]{1,0:T(8,128)(2,1)}, bf16[256,2048]{1,0:T(8,128)(2,1)}) fusion(f32[256,2048]{1,0:T(8,128)} %get-tuple-element.4, f32[2048]{0:T(1024)S(1)} %copy-done, f32[256]{0:T(256)S(1)} %add_rsqrt_fusion), kind=kLoop, calls=%fused_computation | loop fusion | flops 2097152 | bytes 4203520 | tf_op jit(solution)/shard_map/convert_element_type | solution.py:416
  (1 shorter events, 0.0 us)
Async XLA Ops:
  0.6 87.7 %copy-start = (f32[2048]{0:T(1024)S(1)}, f32[2048]{0:T(1024)}, u32[]{:S(2)}) copy-start(f32[2048]{0:T(1024)} %param.13) | copy-start | bytes 24580
